TPU v7x, 32 devices: a whole 2x2x4 slice. The times are simulated.
32 devices in a mesh: grp: 4 (over z), shard: 8 (over y, x, core).
Axes of the slice: x: 2, y: 2, z: 4, core: 2. Of those that a mesh axis runs over, the one named last changes fastest.
Arguments:
- frames_in: float32 [128, 256, 768], P(('grp', 'shard')), may hold values from -6 to 6
- cotangent: float32 [128, 256, 768], P(('grp', 'shard')), may hold values from -6 to 6
- time_table: bfloat16 [1000, 768], P(None, 'shard'), may hold values from -6 to 6
- ada_weight: bfloat16 [768, 6912], P('shard'), may hold values from -0.21875 to 0.21875
- ada_bias: bfloat16 [6912], P('shard'), may hold values from -4 to 4
- space_qkv: bfloat16 [768, 2304], P('shard'), may hold values from -0.21875 to 0.21875
- space_out: bfloat16 [768, 768], P('shard'), may hold values from -2.5 to 2.5
- time_qkv: bfloat16 [768, 2304], P('shard'), may hold values from -0.21875 to 0.21875
- time_out: bfloat16 [768, 768], P('shard'), may hold values from -0.875 to 0.875
- up_weight: bfloat16 [768, 3072], P('shard'), may hold values from -0.21875 to 0.21875
- up_bias: bfloat16 [3072], P('shard'), may hold values from -6 to 6
- down_weight: bfloat16 [3072, 768], P('shard'), may hold values from -0.109375 to 0.109375
- down_bias: bfloat16 [768], P('shard'), may hold values from -4 to 4
- timesteps: int32 [8], P('grp'), may hold values from 0 to 999
- task_mask: int32 [8, 16], P('grp'), may hold values 0 or 1
- clip_weight: float32 [8], P('grp'), may hold values from 0.5 to 2
- frame_table: int32 [4, 32], P('grp'), may hold values from 0 to 31, each once within a row
Outputs:
- frames_out: float32 [128, 256, 768], P(('grp', 'shard'))
- grad_frames_in: float32 [128, 256, 768], P(('grp', 'shard'))
- grad_time_table: float32 [1000, 768], P(None, 'shard')
- grad_ada_weight: float32 [768, 6912], P('shard')
- grad_ada_bias: float32 [6912], P('shard')
- grad_space_qkv: float32 [768, 2304], P('shard')
- grad_space_out: float32 [768, 768], P('shard')
- grad_time_qkv: float32 [768, 2304], P('shard')
- grad_time_out: float32 [768, 768], P('shard')
- grad_up_weight: float32 [768, 3072], P('shard')
- grad_up_bias: float32 [3072], P('shard')
- grad_down_weight: float32 [3072, 768], P('shard')
- grad_down_bias: float32 [768], P('shard')
Inputs may be any that keep to these rules, and one draw needn't show every extreme that they name: `frame_table`: each row lists every frame of its group once.
All inputs are finite; a program needn't handle non-finite values. No bound on the sum of `task_mask` on one device may be relied on, other than what follows from the above.
Results may differ from a plain program's by a relative error of at most 0.014.
Values may be sent and summed in bfloat16 or wider, within the bound.
No kernel may reach another device: no remote copies, remote signals or barrier semaphores. Data moves between devices by JAX's collectives and lax.ppermute only.
A program may use at most 256 MiB of HBM per device.

v0:
```python
from functools import partial
import jax
import jax.numpy as jnp
from jax import lax
from jax.sharding import PartitionSpec as P

HEADS = 12
HEAD_DIM = 64
HIGH = lax.Precision.HIGHEST
EPSILON = 1e-06


def layer_norm(values):
    center = values - jnp.mean(values, axis=-1, keepdims=True)
    spread = jnp.mean(center * center, axis=-1, keepdims=True)
    inverse = lax.rsqrt(spread + EPSILON)
    return (center * inverse, inverse)


def norm_back(grad_normed, normed, inverse):
    first = jnp.mean(grad_normed, axis=-1, keepdims=True)
    second = jnp.mean(grad_normed * normed, axis=-1, keepdims=True)
    return inverse * (grad_normed - first - normed * second)


def split_heads(packed, width):
    shape = packed.shape[:-1] + (HEADS, HEAD_DIM)
    return (
        packed[..., :width].reshape(shape),
        packed[..., width : 2 * width].reshape(shape),
        packed[..., 2 * width :].reshape(shape),
    )


def attend_forward(packed):
    width = packed.shape[-1] // 3
    query, keys, values = split_heads(packed, width)
    scores = jnp.einsum(
        "blmhe,bkmhe->bmhlk", query, keys, preferred_element_type=jnp.float32
    ) * HEAD_DIM ** (-0.5)
    highest = jnp.max(scores, axis=-1, keepdims=True)
    logsum = highest + jnp.log(jnp.sum(jnp.exp(scores - highest), axis=-1, keepdims=True))
    probs = jnp.exp(scores - logsum).astype(jnp.bfloat16)
    mixed = jnp.einsum("bmhlk,bkmhe->blmhe", probs, values, preferred_element_type=jnp.float32)
    return (mixed.reshape(packed.shape[:-1] + (width,)).astype(jnp.bfloat16), logsum)


def attend_backward(packed, logsum, grad_mixed):
    width = packed.shape[-1] // 3
    query, keys, values = split_heads(packed, width)
    factor = HEAD_DIM ** (-0.5)
    scores = (
        jnp.einsum("blmhe,bkmhe->bmhlk", query, keys, preferred_element_type=jnp.float32) * factor
    )
    probs = jnp.exp(scores - logsum)
    grad_heads = grad_mixed.reshape(query.shape)
    grad_probs = jnp.einsum(
        "blmhe,bkmhe->bmhlk", grad_heads, values, preferred_element_type=jnp.float32
    )
    grad_values = jnp.einsum(
        "bmhlk,blmhe->bkmhe",
        probs.astype(jnp.bfloat16),
        grad_heads,
        preferred_element_type=jnp.float32,
    )
    grad_scores = (
        probs * (grad_probs - jnp.sum(probs * grad_probs, axis=-1, keepdims=True))
    ).astype(jnp.bfloat16)
    grad_query = (
        jnp.einsum("bmhlk,bkmhe->blmhe", grad_scores, keys, preferred_element_type=jnp.float32)
        * factor
    )
    grad_keys = (
        jnp.einsum("bmhlk,blmhe->bkmhe", grad_scores, query, preferred_element_type=jnp.float32)
        * factor
    )
    shape = packed.shape[:-1] + (width,)
    joined = jnp.concatenate(
        [grad_query.reshape(shape), grad_keys.reshape(shape), grad_values.reshape(shape)], axis=-1
    )
    return joined.astype(jnp.bfloat16)


def mixer_forward(resid, shift, scale, gate, qkv_weight, out_weight):
    normed, inverse = layer_norm(resid)
    entry = (normed * (1.0 + scale) + shift).astype(jnp.bfloat16)
    packed = jnp.einsum(
        "blmd,de->blme", entry, qkv_weight, preferred_element_type=jnp.float32
    ).astype(jnp.bfloat16)
    mixed, logsum = attend_forward(packed)
    branch = jnp.einsum("blmd,de->blme", mixed, out_weight, preferred_element_type=jnp.float32)
    return (resid + gate * branch, (normed, inverse, entry, packed, logsum, mixed, branch))


def mixer_backward(grad_out, scale, gate, qkv_weight, out_weight, kept, per_clip):
    normed, inverse, entry, packed, logsum, mixed, branch = kept
    grad_gate = per_clip(grad_out * branch)
    grad_branch = (gate * grad_out).astype(jnp.bfloat16)
    grad_outw = jnp.einsum("blmd,blme->de", mixed, grad_branch, preferred_element_type=jnp.float32)
    grad_mixed = jnp.einsum(
        "blme,de->blmd", grad_branch, out_weight, preferred_element_type=jnp.float32
    ).astype(jnp.bfloat16)
    grad_packed = attend_backward(packed, logsum, grad_mixed)
    grad_qkvw = jnp.einsum("blmd,blme->de", entry, grad_packed, preferred_element_type=jnp.float32)
    grad_entry = jnp.einsum(
        "blme,de->blmd", grad_packed, qkv_weight, preferred_element_type=jnp.float32
    )
    grad_shift = per_clip(grad_entry)
    grad_scale = per_clip(grad_entry * normed)
    grad_in = grad_out + norm_back(grad_entry * (1.0 + scale), normed, inverse)
    return (grad_in, (grad_shift, grad_scale, grad_gate), grad_qkvw, grad_outw)


def feed_forward(resid, shift, scale, gate, up_full, up_bias_full, down_full, down_bias_full):
    normed, inverse = layer_norm(resid)
    entry = (normed * (1.0 + scale) + shift).astype(jnp.bfloat16)
    upward = jnp.einsum(
        "blmd,df->blmf", entry, up_full, preferred_element_type=jnp.float32
    ) + up_bias_full.astype(jnp.float32)
    active = jax.nn.gelu(upward, approximate=False).astype(jnp.bfloat16)
    downward = jnp.einsum(
        "blmf,fd->blmd", active, down_full, preferred_element_type=jnp.float32
    ) + down_bias_full.astype(jnp.float32)
    return (resid + gate * downward, (normed, inverse, entry, upward, active, downward))


def feed_backward(grad_out, scale, gate, up_full, down_full, kept, per_clip):
    normed, inverse, entry, upward, active, downward = kept
    grad_gate = per_clip(grad_out * downward)
    grad_down_in = (gate * grad_out).astype(jnp.bfloat16)
    grad_down = jnp.einsum(
        "blmf,blmd->fd", active, grad_down_in, preferred_element_type=jnp.float32
    )
    grad_down_bias = jnp.sum(grad_down_in.astype(jnp.float32), axis=(0, 1, 2))
    grad_active = jnp.einsum(
        "blmd,fd->blmf", grad_down_in, down_full, preferred_element_type=jnp.float32
    )
    _, gelu_back = jax.vjp(partial(jax.nn.gelu, approximate=False), upward)
    grad_up_in = gelu_back(grad_active)[0].astype(jnp.bfloat16)
    grad_up = jnp.einsum("blmd,blmf->df", entry, grad_up_in, preferred_element_type=jnp.float32)
    grad_up_bias = jnp.sum(grad_up_in.astype(jnp.float32), axis=(0, 1, 2))
    grad_entry = jnp.einsum(
        "blmf,df->blmd", grad_up_in, up_full, preferred_element_type=jnp.float32
    )
    grad_shift = per_clip(grad_entry)
    grad_scale = per_clip(grad_entry * normed)
    grad_in = grad_out + norm_back(grad_entry * (1.0 + scale), normed, inverse)
    return (
        grad_in,
        (grad_shift, grad_scale, grad_gate),
        grad_up,
        grad_up_bias,
        grad_down,
        grad_down_bias,
    )


def body(
    frames_in,
    cotangent,
    time_table,
    ada_weight,
    ada_bias,
    space_qkv,
    space_out,
    time_qkv,
    time_out,
    up_weight,
    up_bias,
    down_weight,
    down_bias,
    timesteps,
    task_mask,
    clip_weight,
    frame_table,
):
    shards = lax.axis_size("shard")
    shard_at = lax.axis_index("shard")
    frame_count, patches, width = frames_in.shape
    clips = timesteps.shape[0]
    frames = task_mask.shape[1]
    table = frame_table[0]
    group_frames = table.shape[0]
    columns = patches // shards
    space_qkv_full = lax.all_gather(space_qkv, "shard", axis=0, tiled=True)
    space_out_full = lax.all_gather(space_out, "shard", axis=0, tiled=True)
    time_qkv_full = lax.all_gather(time_qkv, "shard", axis=0, tiled=True)
    time_out_full = lax.all_gather(time_out, "shard", axis=0, tiled=True)
    up_full = lax.all_gather(up_weight, "shard", axis=0, tiled=True)
    down_full = lax.all_gather(down_weight, "shard", axis=0, tiled=True)
    embed = jnp.take(time_table, timesteps, axis=0).astype(jnp.float32)
    cond = jax.nn.silu(embed).astype(jnp.bfloat16)
    mod_local = jnp.dot(cond, ada_weight, preferred_element_type=jnp.float32)

    def spread(local):
        full = jnp.zeros((shards, local.shape[0]), jnp.float32)
        return lax.dynamic_update_slice_in_dim(
            full, local.astype(jnp.float32)[None], shard_at, 0
        ).reshape(-1)

    small = jnp.concatenate(
        [(mod_local + spread(ada_bias)[None]).reshape(-1), spread(up_bias), spread(down_bias)]
    )
    small = lax.psum(small, "shard")
    modul = small[: clips * 9 * width].reshape(clips, 9 * width)
    up_bias_full = small[clips * 9 * width : -width]
    down_bias_full = small[-width:]
    slot_ids = shard_at * frame_count + jnp.arange(frame_count, dtype=jnp.int32)
    frame_ids = jnp.take(table, slot_ids)
    clip_of = frame_ids // frames
    frame_of = frame_ids % frames
    clip_hot = (clip_of[:, None] == jnp.arange(clips, dtype=jnp.int32)[None, :]).astype(jnp.float32)
    frame_mod = jnp.take(modul, clip_of, axis=0)
    own_parts = [
        frame_mod[:, part_at * width : (part_at + 1) * width][:, None, None, :]
        for part_at in range(9)
    ]
    all_parts = [
        modul[:, part_at * width : (part_at + 1) * width][:, None, None, :] for part_at in range(9)
    ]
    inverse = (
        jnp.zeros((group_frames,), jnp.int32)
        .at[table]
        .set(jnp.arange(group_frames, dtype=jnp.int32))
    )

    def frame_sums(values):
        return jnp.dot(clip_hot.T, jnp.sum(values, axis=(1, 2)), precision=HIGH)

    def column_sums(values):
        return jnp.sum(values, axis=(1, 2))

    def to_columns(rows):
        parts = rows.astype(jnp.bfloat16).reshape(frame_count, shards, columns, width)
        parts = jnp.swapaxes(parts, 0, 1)
        moved = lax.all_to_all(parts, "shard", split_axis=0, concat_axis=0, tiled=True)
        return moved.reshape(group_frames, columns, width)

    def to_frames(cols):
        parts = cols.astype(jnp.bfloat16).reshape(shards, frame_count, columns, width)
        moved = lax.all_to_all(parts, "shard", split_axis=0, concat_axis=0, tiled=True)
        moved = jnp.swapaxes(moved, 0, 1)
        return moved.reshape(frame_count, patches, width).astype(jnp.float32)

    space_rows = frames_in.reshape(frame_count, patches, 1, width)
    after_space, space_kept = mixer_forward(
        space_rows, own_parts[0], own_parts[1], own_parts[2], space_qkv_full, space_out_full
    )
    received = to_columns(after_space.reshape(frame_count, patches, width))
    columned = jnp.take(received, inverse, axis=0).reshape(clips, frames, columns, width)
    columned = columned.astype(jnp.float32)
    after_time, time_kept = mixer_forward(
        columned, all_parts[3], all_parts[4], all_parts[5], time_qkv_full, time_out_full
    )
    result, mlp_kept = feed_forward(
        after_time,
        all_parts[6],
        all_parts[7],
        all_parts[8],
        up_full,
        up_bias_full,
        down_full,
        down_bias_full,
    )
    leaving = jnp.take(result.reshape(group_frames, columns, width), table, axis=0)
    frames_out = to_frames(leaving)
    row_weights = task_mask[clip_of, frame_of].astype(jnp.float32) * clip_weight[clip_of]
    weighted = cotangent * row_weights[:, None, None]
    arriving = to_columns(weighted)
    grad_result = jnp.take(arriving, inverse, axis=0).reshape(clips, frames, columns, width)
    grad_result = grad_result.astype(jnp.float32)
    grad_after_time, mlp_mods, grad_up, grad_up_bias, grad_down, grad_down_bias = feed_backward(
        grad_result, all_parts[7], all_parts[8], up_full, down_full, mlp_kept, column_sums
    )
    grad_columned, time_mods, grad_time_qkv, grad_time_out = mixer_backward(
        grad_after_time,
        all_parts[4],
        all_parts[5],
        time_qkv_full,
        time_out_full,
        time_kept,
        column_sums,
    )
    going = jnp.take(grad_columned.reshape(group_frames, columns, width), table, axis=0)
    grad_space = to_frames(going)
    grad_rows, space_mods, grad_space_qkv, grad_space_out = mixer_backward(
        grad_space.reshape(frame_count, patches, 1, width),
        own_parts[1],
        own_parts[2],
        space_qkv_full,
        space_out_full,
        space_kept,
        frame_sums,
    )
    mod_part = jnp.concatenate(space_mods + time_mods + mlp_mods, axis=1)
    small_grads = jnp.concatenate([mod_part.reshape(-1), grad_up_bias, grad_down_bias])
    small_grads = lax.psum(small_grads, "shard")
    mod_size = clips * 9 * width
    grad_modul = small_grads[:mod_size].reshape(clips, 9 * width).astype(jnp.bfloat16)
    up_dev = up_bias.shape[0]
    down_dev = down_bias.shape[0]
    bias_dev = ada_bias.shape[0]
    every_modul = lax.all_gather(grad_modul, "grp", axis=0, tiled=True)
    bias_sums = lax.psum(
        jnp.concatenate(
            [
                lax.dynamic_slice_in_dim(small_grads, mod_size + shard_at * up_dev, up_dev, 0),
                lax.dynamic_slice_in_dim(
                    small_grads, mod_size + shards * up_dev + shard_at * down_dev, down_dev, 0
                ),
            ]
        ),
        "grp",
    )
    every_embed = lax.all_gather(embed.astype(jnp.bfloat16), "grp", axis=0, tiled=True)
    every_embed = every_embed.astype(jnp.float32)
    groups = lax.axis_size("grp")
    step_slots = jnp.zeros((groups, clips), jnp.float32)
    step_slots = lax.dynamic_update_slice_in_dim(
        step_slots, timesteps.astype(jnp.float32)[None], lax.axis_index("grp"), 0
    )
    every_steps = lax.psum(step_slots.reshape(-1), "grp").astype(jnp.int32)
    every_cond = jax.nn.silu(every_embed).astype(jnp.bfloat16)
    grad_ada = jnp.einsum("cd,cj->dj", every_cond, every_modul, preferred_element_type=jnp.float32)
    grad_ada_bias = lax.dynamic_slice_in_dim(
        jnp.sum(every_modul.astype(jnp.float32), axis=0), shard_at * bias_dev, bias_dev, 0
    )
    grad_cond = jnp.einsum("cj,dj->cd", every_modul, ada_weight, preferred_element_type=jnp.float32)
    _, silu_back = jax.vjp(jax.nn.silu, every_embed)
    grad_embed = silu_back(grad_cond)[0]
    vocab = time_table.shape[0]
    onehot = (jnp.arange(vocab, dtype=jnp.int32)[:, None] == every_steps[None, :]).astype(
        jnp.float32
    )
    grad_table = jnp.dot(onehot, grad_embed, precision=HIGH)

    def total(parts):
        flat = [part.astype(jnp.bfloat16).reshape(shards, -1, width) for part in parts]
        rows = [part.shape[1] for part in flat]
        packed = jnp.concatenate(flat, axis=1)
        share = lax.psum_scatter(packed, "shard", scatter_dimension=0, tiled=True)[0]
        share = lax.psum(share, "grp").astype(jnp.float32)
        out, at = ([], 0)
        for part, count in zip(parts, rows):
            piece = share[at : at + count].reshape(part.shape[0] // shards, part.shape[1])
            out.append(piece)
            at += count
        return out

    grad_up, grad_down = total([grad_up, grad_down])
    grad_time_qkv, grad_time_out = total([grad_time_qkv, grad_time_out])
    grad_space_qkv, grad_space_out = total([grad_space_qkv, grad_space_out])
    return (
        frames_out,
        grad_rows.reshape(frame_count, patches, width),
        grad_table,
        grad_ada,
        grad_ada_bias,
        grad_space_qkv,
        grad_space_out,
        grad_time_qkv,
        grad_time_out,
        grad_up,
        bias_sums[:up_dev],
        grad_down,
        bias_sums[up_dev:],
    )


def solution(mesh):
    placed = (
        P(("grp", "shard"), None, None),
        P(("grp", "shard"), None, None),
        P(None, "shard"),
        P("shard", None),
        P("shard"),
        P("shard", None),
        P("shard", None),
        P("shard", None),
        P("shard", None),
        P("shard", None),
        P("shard"),
        P("shard", None),
        P("shard"),
        P("grp"),
        P("grp", None),
        P("grp"),
        P("grp", None),
    )
    return jax.shard_map(
        body,
        mesh=mesh,
        in_specs=placed,
        out_specs=(
            P(("grp", "shard"), None, None),
            P(("grp", "shard"), None, None),
            P(None, "shard"),
            P("shard", None),
            P("shard"),
            P("shard", None),
            P("shard", None),
            P("shard", None),
            P("shard", None),
            P("shard", None),
            P("shard"),
            P("shard", None),
            P("shard"),
        ),
        check_vma=False,
    )
```

profile of v0, /device:TPU:0, one launch (start us, length us, event | category | flops | bytes accessed | tf_op | source)
XLA Modules:
  0.0 886.2 jit_solution(1337077079453278443)
XLA Ops:
  24.4 5.2 all-to-all-start.2
  34.7 35.1 %all-reduce.6.cloned.1.call-done = f32[17664]{0:T(1024)} async-done(((f32[17664]{0:T(1024)}), f32[17664]{0:T(1024)}) %all-reduce.6.cloned.1.call-update) | async-done | bytes 70672 | tf_op jit(solution)/shard_map/psum | solution.py:204
  71.3 35.3 %all-gather.9.cloned.1.call-done = bf16[768,2304]{1,0:T(8,128)(2,1)} async-done(((bf16[96,2304]{1,0:T(8,128)(2,1)}), bf16[768,2304]{1,0:T(8,128)(2,1)}) %all-gather.9.cloned.1.call-update) | async-done | bytes 3538960 | tf_op jit(solution)/shard_map/all_gather | solution.py:185
  106.7 7.0 fusion.9
  119.1 3.8 multiply_reduce_fusion.1
  129.4 8.7 convolution_convert_fusion.3
  138.1 5.9 add_convert_fusion.3
  145.2 3.6 all-to-all-start
  156.2 23.0 %all-to-all-done = bf16[8,4,32,768]{3,2,1,0:T(8,128)(2,1)S(1)} async-done(((bf16[8,4,32,768]{3,2,1,0:T(8,128)(2,1)}), bf16[8,4,32,768]{3,2,1,0:T(8,128)(2,1)S(1)}, u32[]{:S(2)}, u32[]{:S(2)}) %all-to-all-start) | async-done | bytes 1572896 | tf_op jit(solution)/shard_map/all_to_all | solution.py:236
  182.4 5.2 select_convert_fusion.2
  189.8 7.0 convolution_convert_fusion
  199.2 6.1 reshape.639
  205.3 5.9 reshape.640
  211.1 5.9 reshape.638
  217.0 8.0 multiply_reduce_fusion.3
  229.5 3.9 convert_bitcast_fusion.2
  233.4 5.0 copy.166
  238.4 6.5 convert_element_type.258
  244.9 5.8 multiply_add_fusion.3
  255.4 11.7 %fusion.8 = (u16[2,32,3072]{2,1,0:T(8,128)(2,1)S(1)}, u16[2,32,3072]{2,1,0:T(8,128)(2,1)S(1)}, f32[2,16,32,3072]{3,2,1,0:T(8,128)S(1)}) fusion(f32[3072]{0:T(1024)S(1)} %slice.149, bf16[768,3072]{1,0:T(8,128)(2,1)} %all-gather.17.cloned.1.call-done, f32[2,16,32,768]{3,2,1,0:T(8,128)} %get-tuple-element.73, f32[2,768]{1,0:T(2,128)S(1)} %get-tuple-element.54, ...), kind=kOutput, calls=%fused_computation.51 | convolution fusion | flops 4879417344 | bytes 21266432 | tf_op jit(solution)/shard_map/blmd,df->blmf/dot_general | solution.py:117
  267.0 4.9 copy-done.30
  272.0 29.8 %multiply_convert_fusion.1 = (bf16[2,16,32,3072]{3,2,1,0:T(8,128)(2,1)}, f32[2,16,32,3072]{3,2,1,0:T(8,128)}) fusion(f32[2,16,32,3072]{3,2,1,0:T(8,128)S(1)} %get-tuple-element.75, f32[3072]{0:T(1024)S(1)} %slice.149, u16[2,32,3072]{2,1,0:T(8,128)(2,1)S(1)} %get-tuple-element.16, u16[2,32,3072]{2,1,0:T(8,128)(2,1)S(1)} %get-tuple-element.15), kind=kLoop, calls=%fused_computation.21 | loop fusion | flops 223346688 | bytes 32256000 | tf_op jit(solution)/shard_map/convert_element_type | solution.py:120
  301.7 19.7 %convert_reduce_fusion = (f32[3072]{0:T(1024)}, bf16[2,16,32,3072]{3,2,1,0:T(8,128)(2,1)}) fusion(f32[2,16,32,3072]{3,2,1,0:T(8,128)} %get-tuple-element.37, bf16[3072,768]{1,0:T(8,128)(2,1)} %all-gather.19.cloned.1.call-done, f32[2,16,32,768]{3,2,1,0:T(8,128)} %bitcast.240, f32[2,768]{1,0:T(2,128)S(1)} %get-tuple-element.55, ...), kind=kOutput, calls=%fused_computation.17 | convolution fusion | flops 4886885376 | bytes 39352320 | tf_op jit(solution)/shard_map/blmd,fd->blmf/dot_general | solution.py:135
  321.4 10.0 %multiply_reduce_fusion.5 = (f32[2,768]{1,0:T(2,128)}, f32[2,16,32]{2,1,0:T(8,128)S(1)}, f32[2,16,32]{2,1,0:T(8,128)S(1)}, f32[2,768]{1,0:T(2,128)}, f32[2,16,32,768]{3,2,1,0:T(8,128)S(1)}) fusion(f32[2,16,32,768]{3,2,1,0:T(8,128)S(1)} %copy-done.10, f32[2,16,32]{2,1,0:T(8,128)S(1)} %add_rsqrt_fusion, f32[2,16,32]{2,1,0:T(8,128)S(1)} %broadcast_multiply_fusion.4, ...), kind=kOutput, calls=%fused_computation.88 | convolution fusion | flops 4838910976 | bytes 17336320 | tf_op jit(solution)/shard_map/blmf,df->blmd/dot_general | solution.py:142
  338.0 6.2 reshape.645
  344.2 13.1 %multiply_reduce_fusion.2 = (f32[2,32,12,16]{3,2,1,0:T(8,128)S(1)}, f32[2,32,12,16,16]{3,4,2,1,0:T(8,128)}) fusion(f32[2,32,12,16,16]{3,4,2,1,0:T(8,128)} %copy-done.5, f32[2,32,12,16]{3,2,1,0:T(8,128)} %copy-done.28, bf16[2,16,32,12,64]{4,3,2,1,0:T(8,128)(2,1)} %reshape.638, bf16[2,16,32,12,64]{4,3,2,1,0:T(8,128)(2,1)} %reshape.645), kind=kOutput, calls=%fused_computation.47 | convolution fusion | flops 25939968 | bytes 4816896 | tf_op jit(solution)/shard_map/blmhe,bkmhe->bmhlk/dot_general | solution.py:57
  357.3 6.7 convert_bitcast_fusion.1
  366.3 4.0 fusion.26
  376.4 5.2 reshape.646
  381.6 5.0 copy.175
  386.6 6.1 reshape.647
  392.7 5.0 copy.177
  397.8 6.1 reshape.648
  408.1 5.8 bitcast_convert_fusion.2
  413.9 6.8 reshape.657
  420.8 4.5 pad_maximum_fusion.3
  425.4 10.9 %multiply_reduce_fusion.7 = (f32[2,768]{1,0:T(2,128)}, f32[2,16,32]{2,1,0:T(8,128)S(1)}, f32[2,16,32]{2,1,0:T(8,128)S(1)}, f32[2,768]{1,0:T(2,128)}, f32[2,16,32,768]{3,2,1,0:T(8,128)}) fusion(f32[2,16,32,768]{3,2,1,0:T(8,128)} %bitcast.258, f32[2,16,32]{2,1,0:T(8,128)S(1)} %bitcast.274, f32[2,16,32]{2,1,0:T(8,128)S(1)} %bitcast.270, ...), kind=kOutput, calls=%fused_computation.90 | convolution fusion | flops 3630951424 | bytes 14583808 | tf_op jit(solution)/shard_map/blme,de->blmd/dot_general | solution.py:105
  436.3 9.3 %multiply_add_fusion.2 = (bf16[2,16,32,768]{3,2,1,0:T(8,128)(2,1)}, f32[2,16,32,768]{3,2,1,0:T(8,128)}) fusion(f32[2,16,32,768]{3,2,1,0:T(8,128)S(1)} %copy-done.11, f32[768]{0:T(1024)S(1)} %copy-done.61, f32[2,768]{1,0:T(2,128)S(1)} %get-tuple-element.55, bf16[2,16,32,3072]{3,2,1,0:T(8,128)(2,1)S(1)} %bitcast.250, ...), kind=kOutput, calls=%fused_computation.103 | convolution fusion | flops 4834983936 | bytes 18883584 | tf_op jit(solution)/shard_map/blmf,fd->blmd/dot_general | solution.py:121
  445.7 3.5 gather_fusion.6
  449.2 4.4 multiply_add_fusion
  453.6 3.5 gather_fusion.8
  457.1 4.1 select_convert_fusion
  461.2 3.7 all-to-all-start.3
  465.0 10.6 %bitcast_convert_fusion.1 = bf16[768,3072]{1,0:T(8,128)(2,1)} fusion(bf16[2,16,32,3072]{3,2,1,0:T(8,128)(2,1)} %get-tuple-element.86, f32[2,16,32,768]{3,2,1,0:T(8,128)} %get-tuple-element.73, f32[2,768]{1,0:T(2,128)S(1)} %copy-done.66, f32[2,768]{1,0:T(2,128)S(1)} %get-tuple-element.53, f32[2,16,32]{2,1,0:T(8,128)S(1)} %add_rsqrt_fusion, ...), kind=kOutput, calls=%fused_computation.39 | convolution fusion | flops 4838129664 | bytes 14176256 | tf_op jit(solution)/shard_map/blmd,blmf->df/dot_general | solution.py:140
  475.6 8.5 reshape.660
  484.1 8.0 all-to-all-done.3
  502.9 8.1 convolution_convert_fusion.2
  513.7 6.9 multiply_reduce_fusion
  520.6 7.6 multiply_convert_fusion
  534.1 6.0 multiply_convert_fusion.6
  542.8 8.8 bitcast_convert_fusion.3
  551.7 6.7 reshape.654
  563.9 8.2 bitcast_convert_fusion
  572.1 6.9 pad_maximum_fusion
  579.1 3.6 all-to-all-start.1
  582.9 3.5 multiply_reduce_fusion.6
  591.2 7.0 multiply_reduce_fusion.8
  602.7 29.1 %reduce-scatter.4.cloned.1.call-done = bf16[1,384,768]{2,1,0:T(8,128)(2,1)} async-done(((bf16[8,384,768]{2,1,0:T(8,128)(2,1)}), bf16[1,384,768]{2,1,0:T(8,128)(2,1)}) %reduce-scatter.4.cloned.1.call-update) | async-done | bytes 589840 | tf_op jit(solution)/shard_map/reduce_scatter | solution.py:341
  631.8 80.2 %reduce-scatter.8.cloned.1.call-done = bf16[1,768,768]{2,1,0:T(8,128)(2,1)} async-done(((bf16[8,768,768]{2,1,0:T(8,128)(2,1)}), bf16[1,768,768]{2,1,0:T(8,128)(2,1)}) %reduce-scatter.8.cloned.1.call-update) | async-done | bytes 1179664 | tf_op jit(solution)/shard_map/reduce_scatter | solution.py:341
  712.2 10.9 %all-gather.1 = bf16[4,2,96]{2,1,0:T(2,128)(2,1)S(1)} all-gather(bf16[1,2,96]{2,1,0:T(2,128)(2,1)S(1)} %fusion.91), channel_id=1, replica_groups=mesh['grp'=4,'shard'=8] {'grp'}, dimensions={0}, use_global_device_ids=true | all-gather | bytes 1920 | tf_op jit(solution)/shard_map/all_gather | solution.py:315
  723.1 42.7 %all-reduce.8.cloned.1.call-done = f32[17664]{0:T(1024)} async-done(((f32[17664]{0:T(1024)}), f32[17664]{0:T(1024)}) %all-reduce.8.cloned.1.call-update) | async-done | bytes 70672 | tf_op jit(solution)/shard_map/psum | solution.py:297
  769.4 12.1 %all-reduce = (f32[8]{0:T(128)S(1)}, f32[480]{0:T(512)S(1)}) all-reduce(f32[8]{0:T(128)S(1)} %reshape.652, f32[480]{0:T(512)S(1)} %pad_maximum_fusion.8), channel_id=1, replica_groups=mesh['grp'=4,'shard'=8] {'grp'}, use_global_device_ids=true, to_apply=%region_20.23 | all-reduce | flops 488 | bytes 3904 | tf_op jit(solution)/shard_map/psum | solution.py:322
  782.9 14.5 %all-gather = bf16[4,2,6912]{2,1,0:T(2,128)(2,1)S(1)} all-gather(bf16[1,2,6912]{2,1,0:T(2,128)(2,1)S(1)} %reshape.753), channel_id=1, replica_groups=mesh['grp'=4,'shard'=8] {'grp'}, dimensions={0}, use_global_device_ids=true | all-gather | bytes 138240 | tf_op jit(solution)/shard_map/all_gather | solution.py:303
  801.9 64.0 %all-reduce.10.cloned.1.call-done = (bf16[384,768]{1,0:T(8,128)(2,1)}, bf16[384,768]{1,0:T(8,128)(2,1)}, bf16[768,768]{1,0:T(8,128)(2,1)}) async-done(((bf16[384,768]{1,0:T(8,128)(2,1)}, bf16[384,768]{1,0:T(8,128)(2,1)}, bf16[768,768]{1,0:T(8,128)(2,1)}), (bf16[384,768]{1,0:T(8,128)(2,1)}, bf16[384,768]{1,0:T(8,128)(2,1)}, bf16[768,768]{1,0:T(8,128)(2,1)})) %all-reduce.10.cloned.1.call-update) | async-done | bytes 2359312 | tf_op jit(solution)/shard_map/psum | solution.py:342
  (338 shorter events, 139.5 us)
Async XLA Ops:
  7.2 7.4 copy-start
  7.2 11.8 %copy-start.2 = (s32[1,32]{1,0:T(1,128)S(1)}, s32[1,32]{1,0:T(1,128)}, u32[]{:S(2)}) copy-start(s32[1,32]{1,0:T(1,128)} %param.37) | copy-start | bytes 388
  7.2 12.4 %copy-start.4 = (s32[2,16]{1,0:T(2,128)S(1)}, s32[2,16]{1,0:T(2,128)}, u32[]{:S(2)}) copy-start(s32[2,16]{1,0:T(2,128)} %param.35) | copy-start | bytes 388
  7.2 13.1 %copy-start.1 = (f32[2]{0:T(128)S(1)}, f32[2]{0:T(128)}, u32[]{:S(2)}) copy-start(f32[2]{0:T(128)} %param.36) | copy-start | bytes 28
  7.2 62.5 %all-reduce.6.cloned.1.call-start = ((), (), s32[]{:S(2)}) async-start(), calls=%async_computation.7 | async-start | bytes 147456 | tf_op jit(solution)/shard_map/psum | solution.py:204
  8.0 15.1 %copy-start.73 = (pred[2]{0:T(512)(128)(4,1)}, pred[2]{0:T(512)(128)(4,1)S(1)}, u32[]{:S(2)}) copy-start(pred[2]{0:T(512)(128)(4,1)S(1)} %compare_and_fusion.2) | copy-start | bytes 10
  14.6 8.6 copy-start.71
  15.7 91.0 %all-gather.9.cloned.1.call-start = ((), (), s32[]{:S(2)}) async-start(), calls=%async_computation.8 | async-start | bytes 3981312 | tf_op jit(solution)/shard_map/all_gather | solution.py:185
  16.5 121.6 %all-gather.11.cloned.1.call-start = ((), (), s32[]{:S(2)}) async-start(), calls=%async_computation.9 | async-start | bytes 1327104 | tf_op jit(solution)/shard_map/all_gather | solution.py:186
  17.2 172.6 %all-gather.13.cloned.1.call-start = ((), (), s32[]{:S(2)}) async-start(), calls=%async_computation.10 | async-start | bytes 3981312 | tf_op jit(solution)/shard_map/all_gather | solution.py:187
  17.8 227.1 %all-gather.15.cloned.1.call-start = ((), (), s32[]{:S(2)}) async-start(), calls=%async_computation.11 | async-start | bytes 1327104 | tf_op jit(solution)/shard_map/all_gather | solution.py:188
  18.4 237.0 %all-gather.17.cloned.1.call-start = ((), (), s32[]{:S(2)}) async-start(), calls=%async_computation.12 | async-start | bytes 5308416 | tf_op jit(solution)/shard_map/all_gather | solution.py:189
  24.4 120.8 %all-to-all-start.2 = ((bf16[8,4,32,768]{3,2,1,0:T(8,128)(2,1)}), bf16[8,4,32,768]{3,2,1,0:T(8,128)(2,1)}, u32[]{:S(2)}, u32[]{:S(2)}) async-start(bf16[8,4,32,768]{3,2,1,0:T(8,128)(2,1)} %copy.168), calls=%async_computation.2 | async-start | bytes 3145728 | tf_op jit(solution)/shard_map/all_to_all | solution.py:236
  32.3 81.4 %copy-start.56 = (f32[4,256]{1,0:T(4,128)}, f32[4,256]{1,0:T(4,128)S(1)}, u32[]{:S(2)}) copy-start(f32[4,256]{1,0:T(4,128)S(1)} %broadcast_multiply_fusion.8) | copy-start | bytes 12292
  34.7 79.1 %copy-start.59 = (f32[4,256]{1,0:T(4,128)}, f32[4,256]{1,0:T(4,128)S(1)}, u32[]{:S(2)}) copy-start(f32[4,256]{1,0:T(4,128)S(1)} %add_rsqrt_fusion.2) | copy-start | bytes 12292
  71.3 42.4 %copy-start.54 = (f32[4,768]{1,0:T(4,128)}, f32[4,768]{1,0:T(4,128)S(1)}, u32[]{:S(2)}) copy-start(f32[4,768]{1,0:T(4,128)S(1)} %get-tuple-element.52) | copy-start | bytes 36868
  71.3 42.4 %copy-start.62 = (f32[4,768]{1,0:T(4,128)}, f32[4,768]{1,0:T(4,128)S(1)}, u32[]{:S(2)}) copy-start(f32[4,768]{1,0:T(4,128)S(1)} %get-tuple-element.51) | copy-start | bytes 36868
  71.3 66.7 %copy-start.52 = (f32[4,768]{1,0:T(4,128)}, f32[4,768]{1,0:T(4,128)S(1)}, u32[]{:S(2)}) copy-start(f32[4,768]{1,0:T(4,128)S(1)} %get-tuple-element.50) | copy-start | bytes 36868
  119.0 3.9 copy-start.21
  122.9 4.5 copy-start.3
  127.4 10.6 %copy-start.43 = (f32[4,12,256]{2,1,0:T(8,128)}, f32[4,12,256]{2,1,0:T(8,128)S(1)}, u32[]{:S(2)}) copy-start(f32[4,12,256]{2,1,0:T(8,128)S(1)} %log_add_fusion.1) | copy-start | bytes 147460
  129.4 8.7 copy-start.25
  145.2 34.0 %all-to-all-start = ((bf16[8,4,32,768]{3,2,1,0:T(8,128)(2,1)}), bf16[8,4,32,768]{3,2,1,0:T(8,128)(2,1)S(1)}, u32[]{:S(2)}, u32[]{:S(2)}) async-start(bf16[8,4,32,768]{3,2,1,0:T(8,128)(2,1)} %bitcast.226), calls=%async_computation | async-start | bytes 3145728 | tf_op jit(solution)/shard_map/all_to_all | solution.py:236
  148.8 153.0 %all-gather.19.cloned.1.call-start = ((), (), s32[]{:S(2)}) async-start(), calls=%async_computation.13 | async-start | bytes 5308416 | tf_op jit(solution)/shard_map/all_gather | solution.py:190
  149.5 453.2 %reduce-scatter.6.cloned.1.call-start = ((), (), s32[]{:S(2)}) async-start(), calls=%async_computation.16 | async-start | bytes 5308416 | tf_op jit(solution)/shard_map/reduce_scatter | solution.py:341
  152.9 102.4 %copy-start.65 = (f32[2,768]{1,0:T(2,128)}, f32[2,768]{1,0:T(2,128)S(1)}, u32[]{:S(2)}) copy-start(f32[2,768]{1,0:T(2,128)S(1)} %get-tuple-element.54) | copy-start | bytes 18436
  182.4 62.6 %copy-start.6 = (bf16[32,32,768]{2,1,0:T(8,128)(2,1)}, bf16[32,32,768]{2,1,0:T(8,128)(2,1)S(1)}, u32[]{:S(2)}) copy-start(bf16[32,32,768]{2,1,0:T(8,128)(2,1)S(1)} %gather_fusion.5) | copy-start | bytes 4718596
  182.4 5.2 copy-start.19
  225.0 4.5 copy-start.15
  229.5 3.9 copy-start.28
  267.0 4.9 copy-start.30
  301.7 19.7 %copy-start.10 = (f32[2,16,32,768]{3,2,1,0:T(8,128)S(1)}, f32[2,16,32,768]{3,2,1,0:T(8,128)}, u32[]{:S(2)}) copy-start(f32[2,16,32,768]{3,2,1,0:T(8,128)} %get-tuple-element.73) | copy-start | bytes 9437188
  321.4 10.0 %copy-start.20 = (bf16[32,32,768]{2,1,0:T(8,128)(2,1)S(1)}, bf16[32,32,768]{2,1,0:T(8,128)(2,1)}, u32[]{:S(2)}) copy-start(bf16[32,32,768]{2,1,0:T(8,128)(2,1)} %gather_fusion.7) | copy-start | bytes 4718596
  338.0 19.4 %slice-start = ((s8[6291456]{0:T(1024)(128)(4,1)}), s8[2097152]{0:T(1024)(128)(4,1)S(1)}, s32[]{:S(2)}) async-start(s8[6291456]{0:T(1024)(128)(4,1)} %bitcast.230), calls=%async_computation.19 | async-start | bytes 4194304
  344.2 13.1 %slice-start.1 = ((s8[6291456]{0:T(1024)(128)(4,1)}), s8[4194304]{0:T(1024)(128)(4,1)S(1)}, s32[]{:S(2)}) async-start(s8[6291456]{0:T(1024)(128)(4,1)} %bitcast.230), calls=%async_computation.20 | async-start | bytes 8388608
  344.2 13.1 %copy-start.29 = (f32[2,32,12,16]{3,2,1,0:T(8,128)S(1)}, f32[2,32,12,16]{3,2,1,0:T(8,128)}, u32[]{:S(2)}) copy-start(f32[2,32,12,16]{3,2,1,0:T(8,128)} %copy-done.28) | copy-start | bytes 147460
  357.3 6.8 copy-start.18
  366.3 4.0 copy-start.17
  413.9 6.8 copy-start.48
  425.3 11.0 %slice-start.2 = ((s8[6291456]{0:T(1024)(128)(4,1)}), s8[2097152]{0:T(1024)(128)(4,1)S(1)}, s32[]{:S(2)}) async-start(s8[6291456]{0:T(1024)(128)(4,1)} %bitcast.249), calls=%async_computation.21 | async-start | bytes 4194304
  425.3 11.0 %copy-start.11 = (f32[2,16,32,768]{3,2,1,0:T(8,128)S(1)}, f32[2,16,32,768]{3,2,1,0:T(8,128)}, u32[]{:S(2)}) copy-start(f32[2,16,32,768]{3,2,1,0:T(8,128)} %get-tuple-element.73) | copy-start | bytes 9437188
  425.3 11.0 %slice-start.3 = ((s8[6291456]{0:T(1024)(128)(4,1)}), s8[4194304]{0:T(1024)(128)(4,1)S(1)}, s32[]{:S(2)}) async-start(s8[6291456]{0:T(1024)(128)(4,1)} %bitcast.249), calls=%async_computation.22 | async-start | bytes 8388608
  425.3 11.0 %copy-start.61 = (f32[768]{0:T(1024)S(1)}, f32[768]{0:T(1024)}, u32[]{:S(2)}) copy-start(f32[768]{0:T(1024)} %slice.150) | copy-start | bytes 9220
  461.2 3.8 copy-start.66
  461.2 30.9 %all-to-all-start.3 = ((bf16[8,4,32,768]{3,2,1,0:T(8,128)(2,1)}), bf16[8,4,32,768]{3,2,1,0:T(8,128)(2,1)S(1)}, u32[]{:S(2)}, u32[]{:S(2)}) async-start(bf16[8,4,32,768]{3,2,1,0:T(8,128)(2,1)} %bitcast.248), calls=%async_computation.3 | async-start | bytes 3145728 | tf_op jit(solution)/shard_map/all_to_all | solution.py:241
  465.0 166.9 %reduce-scatter.4.cloned.1.call-start = ((), (), s32[]{:S(2)}) async-start(), calls=%async_computation.15 | async-start | bytes 5308416 | tf_op jit(solution)/shard_map/reduce_scatter | solution.py:341
  475.6 16.5 %copy-start.53 = (f32[4,768]{1,0:T(4,128)S(1)}, f32[4,768]{1,0:T(4,128)}, u32[]{:S(2)}) copy-start(f32[4,768]{1,0:T(4,128)} %copy-done.52) | copy-start | bytes 36868
  520.6 7.6 copy-start.23
  551.7 6.7 copy-start.38
  563.9 148.1 %reduce-scatter.8.cloned.1.call-start = ((), (), s32[]{:S(2)}) async-start(), calls=%async_computation.17 | async-start | bytes 10616832 | tf_op jit(solution)/shard_map/reduce_scatter | solution.py:341
  579.1 188.3 %all-to-all-start.1 = ((bf16[8,4,32,768]{3,2,1,0:T(8,128)(2,1)}), bf16[8,4,32,768]{3,2,1,0:T(8,128)(2,1)S(1)}, u32[]{:S(2)}, u32[]{:S(2)}) async-start(bf16[8,4,32,768]{3,2,1,0:T(8,128)(2,1)} %bitcast.32), calls=%async_computation.1 | async-start | bytes 3145728 | tf_op jit(solution)/shard_map/all_to_all | solution.py:241
  582.7 183.1 %all-reduce.8.cloned.1.call-start = ((), (), s32[]{:S(2)}) async-start(), calls=%async_computation.14 | async-start | bytes 147456 | tf_op jit(solution)/shard_map/psum | solution.py:297
  582.9 4.5 copy-start.32
  582.9 5.5 copy-start.40
  591.2 7.1 copy-start.77
  591.2 7.6 copy-start.14
  591.2 7.6 copy-start.31
  598.9 113.1 %copy-start.76 = (f32[1,2]{1,0:T(1,128)S(1)}, f32[1,2]{1,0:T(1,128)}, u32[]{:S(2)}) copy-start(f32[1,2]{1,0:T(1,128)} %get-tuple-element.59) | copy-start | bytes 28
  598.9 113.2 %copy-start.72 = (bf16[2,96]{1,0:T(2,128)(2,1)S(1)}, bf16[2,96]{1,0:T(2,128)(2,1)}, u32[]{:S(2)}) copy-start(bf16[2,96]{1,0:T(2,128)(2,1)} %copy-done.71) | copy-start | bytes 1156
  598.9 113.2 %copy-start.74 = (pred[2]{0:T(512)(128)(4,1)S(1)}, pred[2]{0:T(512)(128)(4,1)}, u32[]{:S(2)}) copy-start(pred[2]{0:T(512)(128)(4,1)} %copy-done.73) | copy-start | bytes 10
  602.7 263.3 %all-reduce.10.cloned.1.call-start = ((), (), s32[]{:S(2)}) async-start(), calls=%async_computation.18 | async-start | bytes 4718592 | tf_op jit(solution)/shard_map/psum | solution.py:342
  781.5 87.3 %copy-start.78 = (f32[480]{0:T(512)}, f32[480]{0:T(512)S(1)}, u32[]{:S(2)}) copy-start(f32[480]{0:T(512)S(1)} %get-tuple-element.32) | copy-start | bytes 5764
  866.0 4.5 copy-start.42
  868.8 6.2 copy-start.39
  (35 other events, 89.2 us)
Sparse Core Ops, SparseCore 0:
  15.8 53.8 all-reduce.5
  71.6 35.0 all-gather.8
  108.6 23.9 all-gather.10
  134.3 43.2 all-gather.12
  179.3 26.1 all-gather.14
  207.3 38.7 all-gather.16
  248.0 38.7 all-gather.18
  425.4 62.8 reduce-scatter.5
  564.0 67.7 reduce-scatter.3
  635.2 76.7 reduce-scatter.7
  715.6 50.1 all-reduce.7
  768.2 97.7 all-reduce.9
where the time goes:
time: 898 us; the launch traced here: 886 us
  waiting for transfers between devices  321 us (36%)
  matrix products  218 us (24%)
  local copies, waits for them, and re-layouts  173 us (19%)
  other arithmetic  103 us (11%)
  blocking collectives  37.5 us (4%)
  starting transfers between devices  16.7 us (2%)
  between operations  15.7 us (2%)
    reduce_scatter x3, waiting for transfers between devices, total(): lax.psum_scatter(packed, 'shard', scatter_dimension=0, tiled=True)[0]  109 us
    psum x1, waiting for transfers between devices, total(): share = lax.psum(share, 'grp').astype(jnp.float32)  64 us
    psum x1, waiting for transfers between devices, body(): small_grads = lax.psum(small_grads, 'shard')  42.7 us
    all_gather x1, waiting for transfers between devices, body(): space_qkv_full = lax.all_gather(space_qkv, 'shard', axis=0, tiled=True)  35.3 us
    psum x1, waiting for transfers between devices, body(): small = lax.psum(small, 'shard')  35.1 us
    convert_element_type x1, other arithmetic, feed_forward(): active = jax.nn.gelu(upward, approximate=False).astype(jnp.bfloat16)  29.8 us
    unnamed x176, local copies, waits for them, and re-layouts  23.9 us
    all_to_all x2, waiting for transfers between devices, to_columns(): lax.all_to_all(parts, 'shard', split_axis=0, concat_axis=0, tiled=True)  23 us
  transfers between devices with their start and end apart: 16, of which 8 were waited for; matrix products, arithmetic and copies ran while one was open for 37% of the time, Pallas kernels for 0%

commit v1 on v0

--- a/solution.py
+++ b/solution.py
@@ -8,6 +8,11 @@
 HEAD_DIM = 64
 HIGH = lax.Precision.HIGHEST
 EPSILON = 1e-06
+
+
+def object_play(sample, mesh_dim="shard"):
+    opened = jnp.sum(lax.all_gather(sample, mesh_dim), axis=0)
+    return opened
 
 
 def layer_norm(values):
@@ -294,7 +299,7 @@
     )
     mod_part = jnp.concatenate(space_mods + time_mods + mlp_mods, axis=1)
     small_grads = jnp.concatenate([mod_part.reshape(-1), grad_up_bias, grad_down_bias])
-    small_grads = lax.psum(small_grads, "shard")
+    small_grads = object_play(small_grads)
     mod_size = clips * 9 * width
     grad_modul = small_grads[:mod_size].reshape(clips, 9 * width).astype(jnp.bfloat16)
     up_dev = up_bias.shape[0]

time: 898 us -> 843 us (0.939)
  waiting for transfers between devices: 321 us -> 259 us
  blocking collectives: 37.5 us -> 47.6 us
    psum x1 -> x0, waiting for transfers between devices: 42.7 us -> none  [body(): small_grads = lax.psum(small_grads, 'shard')]
    reduce_scatter x3, waiting for transfers between devices: 109 us -> 99 us  [total(): lax.psum_scatter(packed, 'shard', scatter_dimension=0, tiled=True)[0]]
    all_gather x0 -> x1, blocking collectives: none -> 9.93 us  [object_play(): opened = jnp.sum(lax.all_gather(sample, mesh_dim), axis=0)]
    psum x1, waiting for transfers between devices: 64 us -> 54.6 us  [total(): share = lax.psum(share, 'grp').astype(jnp.float32)]
    unnamed x176 -> x177, local copies, waits for them, and re-layouts: 23.9 us -> 24 us
  transfers between devices with their start and end apart: 16 -> 15, of which waited for: 8 -> 7; matrix products, arithmetic and copies ran while one was open for 37% -> 40% of each run, Pallas kernels for 0% -> 0%
where the time goes in v1:
time: 843 us; the launch traced here: 831 us
  waiting for transfers between devices  259 us (31%)
  matrix products  218 us (26%)
  local copies, waits for them, and re-layouts  171 us (20%)
  other arithmetic  103 us (12%)
  blocking collectives  47.6 us (6%)
  starting transfers between devices  16.7 us (2%)
  between operations  15.4 us (2%)
    reduce_scatter x3, waiting for transfers between devices, total(): lax.psum_scatter(packed, 'shard', scatter_dimension=0, tiled=True)[0]  99 us
    psum x1, waiting for transfers between devices, total(): share = lax.psum(share, 'grp').astype(jnp.float32)  54.6 us
    all_gather x1, waiting for transfers between devices, body(): space_qkv_full = lax.all_gather(space_qkv, 'shard', axis=0, tiled=True)  35.3 us
    psum x1, waiting for transfers between devices, body(): small = lax.psum(small, 'shard')  35 us
    convert_element_type x1, other arithmetic, feed_forward(): active = jax.nn.gelu(upward, approximate=False).astype(jnp.bfloat16)  29.8 us
    unnamed x177, local copies, waits for them, and re-layouts  24 us
    all_to_all x2, waiting for transfers between devices, to_columns(): lax.all_to_all(parts, 'shard', split_axis=0, concat_axis=0, tiled=True)  23 us
    reshape x3, local copies, waits for them, and re-layouts, total(): part.astype(jnp.bfloat16).reshape(shards, -1, width)  22 us
  transfers between devices with their start and end apart: 15, of which 7 were waited for; matrix products, arithmetic and copies ran while one was open for 40% of the time, Pallas kernels for 0%

profile of v1, /device:TPU:0, one launch (start us, length us, event | category | flops | bytes accessed | tf_op | source)
XLA Modules:
  0.0 831.3 jit_solution(50736343671714944)
XLA Ops:
  24.4 5.2 all-to-all-start.2
  34.7 35.0 %all-reduce.5.cloned.1.call-done = f32[17664]{0:T(1024)} async-done(((f32[17664]{0:T(1024)}), f32[17664]{0:T(1024)}) %all-reduce.5.cloned.1.call-update) | async-done | bytes 70672 | tf_op jit(solution)/shard_map/psum | solution.py:209
  71.3 35.3 %all-gather.11.cloned.1.call-done = bf16[768,2304]{1,0:T(8,128)(2,1)} async-done(((bf16[96,2304]{1,0:T(8,128)(2,1)}), bf16[768,2304]{1,0:T(8,128)(2,1)}) %all-gather.11.cloned.1.call-update) | async-done | bytes 3538960 | tf_op jit(solution)/shard_map/all_gather | solution.py:190
  106.7 7.0 fusion.9
  119.1 3.8 multiply_reduce_fusion.1
  129.4 8.7 %convolution_convert_fusion.3 = bf16[4,12,64,256]{3,2,1,0:T(8,128)(2,1)} fusion(bf16[4,256,12,64]{1,3,2,0:T(8,128)(2,1)S(1)} %bitcast.236, f32[4,12,256,256]{2,3,1,0:T(8,128)} %copy-done.3, f32[4,12,256]{2,1,0:T(8,128)S(1)} %log_add_fusion.1), kind=kOutput, calls=%fused_computation.132 | convolution fusion | flops 412876800 | bytes 15777792 | tf_op jit(solution)/shard_map/bmhlk,bkmhe->blmhe/dot_general | solution.py:49
  138.1 5.9 add_convert_fusion.3
  145.2 3.6 all-to-all-start
  156.2 23.0 %all-to-all-done = bf16[8,4,32,768]{3,2,1,0:T(8,128)(2,1)S(1)} async-done(((bf16[8,4,32,768]{3,2,1,0:T(8,128)(2,1)}), bf16[8,4,32,768]{3,2,1,0:T(8,128)(2,1)S(1)}, u32[]{:S(2)}, u32[]{:S(2)}) %all-to-all-start) | async-done | bytes 1572896 | tf_op jit(solution)/shard_map/all_to_all | solution.py:241
  182.4 5.2 select_convert_fusion.2
  189.8 7.0 convolution_convert_fusion
  199.2 6.1 reshape.639
  205.2 5.9 reshape.640
  211.1 5.9 reshape.638
  217.1 8.0 multiply_reduce_fusion.3
  229.5 3.9 convert_bitcast_fusion.2
  233.5 4.9 copy.166
  238.4 6.5 convert_element_type.258
  244.9 5.8 multiply_add_fusion.3
  255.4 11.6 %fusion.8 = (u16[2,32,3072]{2,1,0:T(8,128)(2,1)S(1)}, u16[2,32,3072]{2,1,0:T(8,128)(2,1)S(1)}, f32[2,16,32,3072]{3,2,1,0:T(8,128)S(1)}) fusion(f32[3072]{0:T(1024)S(1)} %slice.149, bf16[768,3072]{1,0:T(8,128)(2,1)} %all-gather.19.cloned.1.call-done, f32[2,16,32,768]{3,2,1,0:T(8,128)} %get-tuple-element.73, f32[2,768]{1,0:T(2,128)S(1)} %get-tuple-element.54, ...), kind=kOutput, calls=%fused_computation.51 | convolution fusion | flops 4879417344 | bytes 21266432 | tf_op jit(solution)/shard_map/blmd,df->blmf/dot_general | solution.py:122
  267.0 4.9 copy-done.30
  271.9 29.8 %multiply_convert_fusion.1 = (bf16[2,16,32,3072]{3,2,1,0:T(8,128)(2,1)}, f32[2,16,32,3072]{3,2,1,0:T(8,128)}) fusion(f32[2,16,32,3072]{3,2,1,0:T(8,128)S(1)} %get-tuple-element.75, f32[3072]{0:T(1024)S(1)} %slice.149, u16[2,32,3072]{2,1,0:T(8,128)(2,1)S(1)} %get-tuple-element.16, u16[2,32,3072]{2,1,0:T(8,128)(2,1)S(1)} %get-tuple-element.15), kind=kLoop, calls=%fused_computation.21 | loop fusion | flops 223346688 | bytes 32256000 | tf_op jit(solution)/shard_map/convert_element_type | solution.py:125
  301.8 19.7 %convert_reduce_fusion = (f32[3072]{0:T(1024)}, bf16[2,16,32,3072]{3,2,1,0:T(8,128)(2,1)}) fusion(f32[2,16,32,3072]{3,2,1,0:T(8,128)} %get-tuple-element.37, bf16[3072,768]{1,0:T(8,128)(2,1)} %all-gather.21.cloned.1.call-done, f32[2,16,32,768]{3,2,1,0:T(8,128)} %bitcast.240, f32[2,768]{1,0:T(2,128)S(1)} %get-tuple-element.55, ...), kind=kOutput, calls=%fused_computation.17 | convolution fusion | flops 4886885376 | bytes 39352320 | tf_op jit(solution)/shard_map/blmd,fd->blmf/dot_general | solution.py:140
  321.4 10.0 %multiply_reduce_fusion.5 = (f32[2,768]{1,0:T(2,128)}, f32[2,16,32]{2,1,0:T(8,128)S(1)}, f32[2,16,32]{2,1,0:T(8,128)S(1)}, f32[2,768]{1,0:T(2,128)}, f32[2,16,32,768]{3,2,1,0:T(8,128)S(1)}) fusion(f32[2,16,32,768]{3,2,1,0:T(8,128)S(1)} %copy-done.10, f32[2,16,32]{2,1,0:T(8,128)S(1)} %add_rsqrt_fusion, f32[2,16,32]{2,1,0:T(8,128)S(1)} %broadcast_multiply_fusion.4, ...), kind=kOutput, calls=%fused_computation.88 | convolution fusion | flops 4838910976 | bytes 17336320 | tf_op jit(solution)/shard_map/blmf,df->blmd/dot_general | solution.py:147
  338.0 6.2 reshape.645
  344.2 13.1 %multiply_reduce_fusion.2 = (f32[2,32,12,16]{3,2,1,0:T(8,128)S(1)}, f32[2,32,12,16,16]{3,4,2,1,0:T(8,128)}) fusion(f32[2,32,12,16,16]{3,4,2,1,0:T(8,128)} %copy-done.5, f32[2,32,12,16]{3,2,1,0:T(8,128)} %copy-done.28, bf16[2,16,32,12,64]{4,3,2,1,0:T(8,128)(2,1)} %reshape.638, bf16[2,16,32,12,64]{4,3,2,1,0:T(8,128)(2,1)} %reshape.645), kind=kOutput, calls=%fused_computation.47 | convolution fusion | flops 25939968 | bytes 4816896 | tf_op jit(solution)/shard_map/blmhe,bkmhe->bmhlk/dot_general | solution.py:62
  357.4 6.7 convert_bitcast_fusion.1
  366.4 4.0 fusion.26
  376.4 5.2 reshape.646
  381.6 5.0 copy.175
  386.7 6.1 reshape.647
  392.8 5.0 copy.177
  397.8 6.1 reshape.648
  408.2 5.8 bitcast_convert_fusion.2
  414.0 6.8 reshape.657
  420.8 4.5 pad_maximum_fusion.3
  425.4 10.9 %multiply_reduce_fusion.7 = (f32[2,768]{1,0:T(2,128)}, f32[2,16,32]{2,1,0:T(8,128)S(1)}, f32[2,16,32]{2,1,0:T(8,128)S(1)}, f32[2,768]{1,0:T(2,128)}, f32[2,16,32,768]{3,2,1,0:T(8,128)}) fusion(f32[2,16,32,768]{3,2,1,0:T(8,128)} %bitcast.258, f32[2,16,32]{2,1,0:T(8,128)S(1)} %bitcast.274, f32[2,16,32]{2,1,0:T(8,128)S(1)} %bitcast.270, ...), kind=kOutput, calls=%fused_computation.90 | convolution fusion | flops 3630951424 | bytes 14583808 | tf_op jit(solution)/shard_map/blme,de->blmd/dot_general | solution.py:110
  436.4 9.3 %multiply_add_fusion.2 = (bf16[2,16,32,768]{3,2,1,0:T(8,128)(2,1)}, f32[2,16,32,768]{3,2,1,0:T(8,128)}) fusion(f32[2,16,32,768]{3,2,1,0:T(8,128)S(1)} %copy-done.11, f32[768]{0:T(1024)S(1)} %copy-done.61, f32[2,768]{1,0:T(2,128)S(1)} %get-tuple-element.55, bf16[2,16,32,3072]{3,2,1,0:T(8,128)(2,1)S(1)} %bitcast.250, ...), kind=kOutput, calls=%fused_computation.103 | convolution fusion | flops 4834983936 | bytes 18883584 | tf_op jit(solution)/shard_map/blmf,fd->blmd/dot_general | solution.py:126
  445.7 3.5 gather_fusion.6
  449.2 4.4 multiply_add_fusion
  453.6 3.5 gather_fusion.8
  457.1 4.1 select_convert_fusion
  461.2 3.7 all-to-all-start.3
  465.0 10.6 %bitcast_convert_fusion.1 = bf16[768,3072]{1,0:T(8,128)(2,1)} fusion(bf16[2,16,32,3072]{3,2,1,0:T(8,128)(2,1)} %get-tuple-element.86, f32[2,16,32,768]{3,2,1,0:T(8,128)} %get-tuple-element.73, f32[2,768]{1,0:T(2,128)S(1)} %copy-done.66, f32[2,768]{1,0:T(2,128)S(1)} %get-tuple-element.53, f32[2,16,32]{2,1,0:T(8,128)S(1)} %add_rsqrt_fusion, ...), kind=kOutput, calls=%fused_computation.39 | convolution fusion | flops 4838129664 | bytes 14176256 | tf_op jit(solution)/shard_map/blmd,blmf->df/dot_general | solution.py:145
  475.6 8.5 %reshape.660 = bf16[8,384,768]{2,1,0:T(8,128)(2,1)} reshape(bf16[768,3072]{1,0:T(8,128)(2,1)} %bitcast_convert_fusion.1) | data formatting | bytes 9437184 | tf_op jit(solution)/shard_map/reshape | solution.py:343
  484.1 8.0 all-to-all-done.3
  502.9 8.1 convolution_convert_fusion.2
  513.7 6.9 multiply_reduce_fusion
  520.6 7.6 multiply_convert_fusion
  534.1 6.0 multiply_convert_fusion.6
  542.9 8.8 %bitcast_convert_fusion.3 = bf16[768,2304]{1,0:T(8,128)(2,1)} fusion(bf16[4,256,768]{2,1,0:T(8,128)(2,1)S(1)} %copy-done.45, bf16[4,256,768]{2,1,0:T(8,128)(2,1)} %copy.184, bf16[4,256,768]{2,1,0:T(8,128)(2,1)} %copy.183, f32[4,256,768]{2,1,0:T(8,128)} %param.21, f32[4,768]{1,0:T(4,128)S(1)} %copy-done.64, f32[4,768]{1,0:T(4,128)S(1)} %copy-done.55, ...), kind=kOutput, calls=%fused_computation.43 | convolution fusion | flops 3643736064 | bytes 11436032 | tf_op jit(solution)/shard_map/blmd,blme->de/dot_general | solution.py:109
  551.7 6.7 reshape.654
  563.9 8.2 bitcast_convert_fusion
  572.2 6.9 pad_maximum_fusion
  579.9 11.0 %all-gather.3 = bf16[4,2,96]{2,1,0:T(2,128)(2,1)S(1)} all-gather(bf16[1,2,96]{2,1,0:T(2,128)(2,1)S(1)} %fusion.91), channel_id=1, replica_groups=mesh['grp'=4,'shard'=8] {'grp'}, dimensions={0}, use_global_device_ids=true | all-gather | bytes 1920 | tf_op jit(solution)/shard_map/all_gather | solution.py:320
  590.9 3.6 all-to-all-start.1
  594.8 3.5 multiply_reduce_fusion.6
  602.5 7.1 multiply_reduce_fusion.8
  613.1 18.8 %reduce-scatter.4.cloned.1.call-done = bf16[1,384,768]{2,1,0:T(8,128)(2,1)} async-done(((bf16[8,384,768]{2,1,0:T(8,128)(2,1)}), bf16[1,384,768]{2,1,0:T(8,128)(2,1)}) %reduce-scatter.4.cloned.1.call-update) | async-done | bytes 589840 | tf_op jit(solution)/shard_map/reduce_scatter | solution.py:346
  631.9 80.2 %reduce-scatter.8.cloned.1.call-done = bf16[1,768,768]{2,1,0:T(8,128)(2,1)} async-done(((bf16[8,768,768]{2,1,0:T(8,128)(2,1)}), bf16[1,768,768]{2,1,0:T(8,128)(2,1)}) %reduce-scatter.8.cloned.1.call-update) | async-done | bytes 1179664 | tf_op jit(solution)/shard_map/reduce_scatter | solution.py:346
  712.4 9.9 %all-gather.1 = f32[8,1,17664]{2,1,0:T(1,128)S(1)} all-gather(f32[1,1,17664]{2,1,0:T(1,128)S(1)} %reshape.754), channel_id=2, replica_groups=mesh['grp'=4,'shard'=8] {'shard'}, dimensions={0}, use_global_device_ids=true | all-gather | bytes 635904 | tf_op jit(solution)/shard_map/all_gather | solution.py:14
  722.9 12.3 %all-reduce = (f32[8]{0:T(128)S(1)}, f32[480]{0:T(512)S(1)}) all-reduce(f32[8]{0:T(128)S(1)} %reshape.652, f32[480]{0:T(512)S(1)} %pad_maximum_fusion.8), channel_id=1, replica_groups=mesh['grp'=4,'shard'=8] {'grp'}, use_global_device_ids=true, to_apply=%region_20.23 | all-reduce | flops 488 | bytes 3904 | tf_op jit(solution)/shard_map/psum | solution.py:327
  735.8 14.4 %all-gather.2 = bf16[4,2,6912]{2,1,0:T(2,128)(2,1)S(1)} all-gather(bf16[1,2,6912]{2,1,0:T(2,128)(2,1)S(1)} %reshape.756), channel_id=1, replica_groups=mesh['grp'=4,'shard'=8] {'grp'}, dimensions={0}, use_global_device_ids=true | all-gather | bytes 138240 | tf_op jit(solution)/shard_map/all_gather | solution.py:308
  756.8 54.6 %all-reduce.7.cloned.1.call-done = (bf16[384,768]{1,0:T(8,128)(2,1)}, bf16[384,768]{1,0:T(8,128)(2,1)}, bf16[768,768]{1,0:T(8,128)(2,1)}) async-done(((bf16[384,768]{1,0:T(8,128)(2,1)}, bf16[384,768]{1,0:T(8,128)(2,1)}, bf16[768,768]{1,0:T(8,128)(2,1)}), (bf16[384,768]{1,0:T(8,128)(2,1)}, bf16[384,768]{1,0:T(8,128)(2,1)}, bf16[768,768]{1,0:T(8,128)(2,1)})) %all-reduce.7.cloned.1.call-update) | async-done | bytes 2359312 | tf_op jit(solution)/shard_map/psum | solution.py:347
  (338 shorter events, 137.1 us)
Async XLA Ops:
  7.2 7.4 copy-start
  7.2 11.8 %copy-start.2 = (s32[1,32]{1,0:T(1,128)S(1)}, s32[1,32]{1,0:T(1,128)}, u32[]{:S(2)}) copy-start(s32[1,32]{1,0:T(1,128)} %param.37) | copy-start | bytes 388
  7.2 12.4 %copy-start.4 = (s32[2,16]{1,0:T(2,128)S(1)}, s32[2,16]{1,0:T(2,128)}, u32[]{:S(2)}) copy-start(s32[2,16]{1,0:T(2,128)} %param.35) | copy-start | bytes 388
  7.2 13.1 %copy-start.1 = (f32[2]{0:T(128)S(1)}, f32[2]{0:T(128)}, u32[]{:S(2)}) copy-start(f32[2]{0:T(128)} %param.36) | copy-start | bytes 28
  7.2 62.5 %all-reduce.5.cloned.1.call-start = ((), (), s32[]{:S(2)}) async-start(), calls=%async_computation.7 | async-start | bytes 147456 | tf_op jit(solution)/shard_map/psum | solution.py:209
  8.0 15.1 %copy-start.73 = (pred[2]{0:T(512)(128)(4,1)}, pred[2]{0:T(512)(128)(4,1)S(1)}, u32[]{:S(2)}) copy-start(pred[2]{0:T(512)(128)(4,1)S(1)} %compare_and_fusion.2) | copy-start | bytes 10
  14.6 8.6 %copy-start.71 = (bf16[2,96]{1,0:T(2,128)(2,1)}, bf16[2,96]{1,0:T(2,128)(2,1)S(1)}, u32[]{:S(2)}) copy-start(bf16[2,96]{1,0:T(2,128)(2,1)S(1)} %gather_fusion.1) | copy-start | bytes 1156
  15.7 91.0 %all-gather.11.cloned.1.call-start = ((), (), s32[]{:S(2)}) async-start(), calls=%async_computation.8 | async-start | bytes 3981312 | tf_op jit(solution)/shard_map/all_gather | solution.py:190
  16.5 121.6 %all-gather.13.cloned.1.call-start = ((), (), s32[]{:S(2)}) async-start(), calls=%async_computation.9 | async-start | bytes 1327104 | tf_op jit(solution)/shard_map/all_gather | solution.py:191
  17.2 172.6 %all-gather.15.cloned.1.call-start = ((), (), s32[]{:S(2)}) async-start(), calls=%async_computation.10 | async-start | bytes 3981312 | tf_op jit(solution)/shard_map/all_gather | solution.py:192
  17.8 227.2 %all-gather.17.cloned.1.call-start = ((), (), s32[]{:S(2)}) async-start(), calls=%async_computation.11 | async-start | bytes 1327104 | tf_op jit(solution)/shard_map/all_gather | solution.py:193
  18.4 237.0 %all-gather.19.cloned.1.call-start = ((), (), s32[]{:S(2)}) async-start(), calls=%async_computation.12 | async-start | bytes 5308416 | tf_op jit(solution)/shard_map/all_gather | solution.py:194
  24.4 120.8 %all-to-all-start.2 = ((bf16[8,4,32,768]{3,2,1,0:T(8,128)(2,1)}), bf16[8,4,32,768]{3,2,1,0:T(8,128)(2,1)}, u32[]{:S(2)}, u32[]{:S(2)}) async-start(bf16[8,4,32,768]{3,2,1,0:T(8,128)(2,1)} %copy.168), calls=%async_computation.2 | async-start | bytes 3145728 | tf_op jit(solution)/shard_map/all_to_all | solution.py:241
  32.3 81.4 %copy-start.56 = (f32[4,256]{1,0:T(4,128)}, f32[4,256]{1,0:T(4,128)S(1)}, u32[]{:S(2)}) copy-start(f32[4,256]{1,0:T(4,128)S(1)} %broadcast_multiply_fusion.8) | copy-start | bytes 12292
  34.7 79.0 %copy-start.59 = (f32[4,256]{1,0:T(4,128)}, f32[4,256]{1,0:T(4,128)S(1)}, u32[]{:S(2)}) copy-start(f32[4,256]{1,0:T(4,128)S(1)} %add_rsqrt_fusion.2) | copy-start | bytes 12292
  71.3 42.4 %copy-start.54 = (f32[4,768]{1,0:T(4,128)}, f32[4,768]{1,0:T(4,128)S(1)}, u32[]{:S(2)}) copy-start(f32[4,768]{1,0:T(4,128)S(1)} %get-tuple-element.52) | copy-start | bytes 36868
  71.3 42.4 %copy-start.63 = (f32[4,768]{1,0:T(4,128)}, f32[4,768]{1,0:T(4,128)S(1)}, u32[]{:S(2)}) copy-start(f32[4,768]{1,0:T(4,128)S(1)} %get-tuple-element.51) | copy-start | bytes 36868
  71.3 66.7 %copy-start.52 = (f32[4,768]{1,0:T(4,128)}, f32[4,768]{1,0:T(4,128)S(1)}, u32[]{:S(2)}) copy-start(f32[4,768]{1,0:T(4,128)S(1)} %get-tuple-element.50) | copy-start | bytes 36868
  119.1 3.9 copy-start.21
  122.9 4.5 copy-start.3
  127.4 10.6 %copy-start.43 = (f32[4,12,256]{2,1,0:T(8,128)}, f32[4,12,256]{2,1,0:T(8,128)S(1)}, u32[]{:S(2)}) copy-start(f32[4,12,256]{2,1,0:T(8,128)S(1)} %log_add_fusion.1) | copy-start | bytes 147460
  129.4 8.7 %copy-start.25 = (bf16[4,256,1,768]{1,3,0,2:T(8,128)(2,1)}, bf16[4,256,1,768]{1,3,0,2:T(8,128)(2,1)S(1)}, u32[]{:S(2)}) copy-start(bf16[4,256,1,768]{1,3,0,2:T(8,128)(2,1)S(1)} %copy.156) | copy-start | bytes 4718596
  145.2 34.0 %all-to-all-start = ((bf16[8,4,32,768]{3,2,1,0:T(8,128)(2,1)}), bf16[8,4,32,768]{3,2,1,0:T(8,128)(2,1)S(1)}, u32[]{:S(2)}, u32[]{:S(2)}) async-start(bf16[8,4,32,768]{3,2,1,0:T(8,128)(2,1)} %bitcast.226), calls=%async_computation | async-start | bytes 3145728 | tf_op jit(solution)/shard_map/all_to_all | solution.py:241
  148.8 153.0 %all-gather.21.cloned.1.call-start = ((), (), s32[]{:S(2)}) async-start(), calls=%async_computation.13 | async-start | bytes 5308416 | tf_op jit(solution)/shard_map/all_gather | solution.py:195
  149.5 463.6 %reduce-scatter.6.cloned.1.call-start = ((), (), s32[]{:S(2)}) async-start(), calls=%async_computation.15 | async-start | bytes 5308416 | tf_op jit(solution)/shard_map/reduce_scatter | solution.py:346
  152.9 102.4 %copy-start.65 = (f32[2,768]{1,0:T(2,128)}, f32[2,768]{1,0:T(2,128)S(1)}, u32[]{:S(2)}) copy-start(f32[2,768]{1,0:T(2,128)S(1)} %get-tuple-element.54) | copy-start | bytes 18436
  182.4 62.6 %copy-start.6 = (bf16[32,32,768]{2,1,0:T(8,128)(2,1)}, bf16[32,32,768]{2,1,0:T(8,128)(2,1)S(1)}, u32[]{:S(2)}) copy-start(bf16[32,32,768]{2,1,0:T(8,128)(2,1)S(1)} %gather_fusion.5) | copy-start | bytes 4718596
  182.4 5.2 copy-start.19
  225.1 4.5 copy-start.15
  229.5 3.9 copy-start.28
  267.0 4.9 copy-start.30
  301.8 19.7 %copy-start.10 = (f32[2,16,32,768]{3,2,1,0:T(8,128)S(1)}, f32[2,16,32,768]{3,2,1,0:T(8,128)}, u32[]{:S(2)}) copy-start(f32[2,16,32,768]{3,2,1,0:T(8,128)} %get-tuple-element.73) | copy-start | bytes 9437188
  321.4 10.0 %copy-start.20 = (bf16[32,32,768]{2,1,0:T(8,128)(2,1)S(1)}, bf16[32,32,768]{2,1,0:T(8,128)(2,1)}, u32[]{:S(2)}) copy-start(bf16[32,32,768]{2,1,0:T(8,128)(2,1)} %gather_fusion.7) | copy-start | bytes 4718596
  338.0 19.4 %slice-start = ((s8[6291456]{0:T(1024)(128)(4,1)}), s8[2097152]{0:T(1024)(128)(4,1)S(1)}, s32[]{:S(2)}) async-start(s8[6291456]{0:T(1024)(128)(4,1)} %bitcast.230), calls=%async_computation.18 | async-start | bytes 4194304
  344.2 13.2 %slice-start.1 = ((s8[6291456]{0:T(1024)(128)(4,1)}), s8[4194304]{0:T(1024)(128)(4,1)S(1)}, s32[]{:S(2)}) async-start(s8[6291456]{0:T(1024)(128)(4,1)} %bitcast.230), calls=%async_computation.19 | async-start | bytes 8388608
  344.2 13.2 %copy-start.29 = (f32[2,32,12,16]{3,2,1,0:T(8,128)S(1)}, f32[2,32,12,16]{3,2,1,0:T(8,128)}, u32[]{:S(2)}) copy-start(f32[2,32,12,16]{3,2,1,0:T(8,128)} %copy-done.28) | copy-start | bytes 147460
  357.4 6.8 copy-start.18
  366.4 4.1 copy-start.17
  414.0 6.8 copy-start.48
  425.3 11.0 %slice-start.2 = ((s8[6291456]{0:T(1024)(128)(4,1)}), s8[2097152]{0:T(1024)(128)(4,1)S(1)}, s32[]{:S(2)}) async-start(s8[6291456]{0:T(1024)(128)(4,1)} %bitcast.249), calls=%async_computation.20 | async-start | bytes 4194304
  425.4 11.0 %copy-start.11 = (f32[2,16,32,768]{3,2,1,0:T(8,128)S(1)}, f32[2,16,32,768]{3,2,1,0:T(8,128)}, u32[]{:S(2)}) copy-start(f32[2,16,32,768]{3,2,1,0:T(8,128)} %get-tuple-element.73) | copy-start | bytes 9437188
  425.4 11.0 %slice-start.3 = ((s8[6291456]{0:T(1024)(128)(4,1)}), s8[4194304]{0:T(1024)(128)(4,1)S(1)}, s32[]{:S(2)}) async-start(s8[6291456]{0:T(1024)(128)(4,1)} %bitcast.249), calls=%async_computation.21 | async-start | bytes 8388608
  425.4 11.0 %copy-start.61 = (f32[768]{0:T(1024)S(1)}, f32[768]{0:T(1024)}, u32[]{:S(2)}) copy-start(f32[768]{0:T(1024)} %slice.150) | copy-start | bytes 9220
  461.2 30.9 %all-to-all-start.3 = ((bf16[8,4,32,768]{3,2,1,0:T(8,128)(2,1)}), bf16[8,4,32,768]{3,2,1,0:T(8,128)(2,1)S(1)}, u32[]{:S(2)}, u32[]{:S(2)}) async-start(bf16[8,4,32,768]{3,2,1,0:T(8,128)(2,1)} %bitcast.248), calls=%async_computation.3 | async-start | bytes 3145728 | tf_op jit(solution)/shard_map/all_to_all | solution.py:246
  464.9 167.0 %reduce-scatter.4.cloned.1.call-start = ((), (), s32[]{:S(2)}) async-start(), calls=%async_computation.14 | async-start | bytes 5308416 | tf_op jit(solution)/shard_map/reduce_scatter | solution.py:346
  475.6 16.5 %copy-start.53 = (f32[4,768]{1,0:T(4,128)S(1)}, f32[4,768]{1,0:T(4,128)}, u32[]{:S(2)}) copy-start(f32[4,768]{1,0:T(4,128)} %copy-done.52) | copy-start | bytes 36868
  520.6 7.6 copy-start.23
  551.7 6.7 copy-start.38
  563.9 148.2 %reduce-scatter.8.cloned.1.call-start = ((), (), s32[]{:S(2)}) async-start(), calls=%async_computation.16 | async-start | bytes 10616832 | tf_op jit(solution)/shard_map/reduce_scatter | solution.py:346
  590.9 163.8 %all-to-all-start.1 = ((bf16[8,4,32,768]{3,2,1,0:T(8,128)(2,1)}), bf16[8,4,32,768]{3,2,1,0:T(8,128)(2,1)S(1)}, u32[]{:S(2)}, u32[]{:S(2)}) async-start(bf16[8,4,32,768]{3,2,1,0:T(8,128)(2,1)} %bitcast.32), calls=%async_computation.1 | async-start | bytes 3145728 | tf_op jit(solution)/shard_map/all_to_all | solution.py:246
  594.5 216.9 %all-reduce.7.cloned.1.call-start = ((), (), s32[]{:S(2)}) async-start(), calls=%async_computation.17 | async-start | bytes 4718592 | tf_op jit(solution)/shard_map/psum | solution.py:347
  594.7 3.9 copy-start.32
  594.8 4.9 copy-start.40
  602.4 7.1 copy-start.77
  602.4 7.7 copy-start.14
  602.5 7.7 copy-start.31
  610.1 102.0 %copy-start.69 = (f32[2,768]{1,0:T(2,128)S(1)}, f32[2,768]{1,0:T(2,128)}, u32[]{:S(2)}) copy-start(f32[2,768]{1,0:T(2,128)} %get-tuple-element.19) | copy-start | bytes 18436
  610.2 102.0 %copy-start.68 = (f32[2,768]{1,0:T(2,128)S(1)}, f32[2,768]{1,0:T(2,128)}, u32[]{:S(2)}) copy-start(f32[2,768]{1,0:T(2,128)} %get-tuple-element.26) | copy-start | bytes 18436
  610.2 102.0 %copy-start.67 = (f32[2,768]{1,0:T(2,128)S(1)}, f32[2,768]{1,0:T(2,128)}, u32[]{:S(2)}) copy-start(f32[2,768]{1,0:T(2,128)} %get-tuple-element.17) | copy-start | bytes 18436
  610.2 102.1 %copy-start.58 = (f32[768]{0:T(1024)S(1)}, f32[768]{0:T(1024)}, u32[]{:S(2)}) copy-start(f32[768]{0:T(1024)} %get-tuple-element.29) | copy-start | bytes 9220
  610.2 102.1 %copy-start.62 = (f32[3072]{0:T(1024)S(1)}, f32[3072]{0:T(1024)}, u32[]{:S(2)}) copy-start(f32[3072]{0:T(1024)} %get-tuple-element.85) | copy-start | bytes 36868
  735.2 21.6 %copy-start.78 = (f32[480]{0:T(512)}, f32[480]{0:T(512)S(1)}, u32[]{:S(2)}) copy-start(f32[480]{0:T(512)S(1)} %get-tuple-element.32) | copy-start | bytes 5764
  811.4 4.5 copy-start.42
  814.2 6.2 copy-start.39
  (34 other events, 80.0 us)
Sparse Core Ops, SparseCore 0:
  15.8 53.8 all-reduce.4
  71.6 35.0 all-gather.10
  108.6 23.9 all-gather.12
  134.3 43.2 all-gather.14
  179.3 26.2 all-gather.16
  207.3 38.7 all-gather.18
  248.0 38.7 all-gather.20
  425.5 62.7 reduce-scatter.5
  564.0 67.8 reduce-scatter.3
  635.2 76.8 reduce-scatter.7
  714.7 96.6 all-reduce.6
